TPU v7x, 256 devices: a whole 4x4x8 slice. The times are simulated.
256 devices in a mesh: seq: 8 (over z), head: 4 (over y_hi, core), rep: 8 (over y_lo, x).
Axes of the slice: x: 4, y: 4 (y_hi: 2, y_lo: 2; y = y_hi * 2 + y_lo), z: 8, core: 2. Of those that a mesh axis runs over, the one named last changes fastest.
Arguments:
- queries: bfloat16 [8, 2048, 7168], P('rep', 'seq', 'head'), may hold values from -6 to 6
- new_keys: bfloat16 [8, 2048, 7168], P('rep', 'seq', 'head'), may hold values from -6 to 6
- new_values: bfloat16 [8, 2048, 7168], P('rep', 'seq', 'head'), may hold values from -4 to 4
- lengths: int32 [8, 4], P('rep'), may hold values from 1 to 1024, 2048 in all within a row
- offsets: int32 [8, 4], P('rep'), may hold values from 0 to 4095
- slot_map: int32 [8, 4], P('rep'), may hold values from 0 to 3, each once within a row
Outputs:
- attended: bfloat16 [8, 2048, 7168], P('rep', 'seq', 'head')
- key_cache: bfloat16 [8, 4, 1024, 7168], P('rep', 'head', None, 'seq')
- value_cache: bfloat16 [8, 4, 1024, 7168], P('rep', 'head', None, 'seq')
Inputs may be any that keep to these rules, and one draw needn't show every extreme that they name: `lengths`: each row sums to 2048; its first entry is the group's shared prompt; every row has one entry equal to 1024. `slot_map`: each row is a permutation of the group's requests.
All inputs are finite; a program needn't handle non-finite values.
Results may differ from a plain program's by a relative error of at most 0.011.
Values may be sent and summed in bfloat16 or wider, within the bound.
A program may use at most 128 MiB of HBM per device.

v0:
```python
import math
import jax
import jax.numpy as jnp
from jax import lax
from jax.sharding import PartitionSpec as P

HD = 224
NEG_FILL = -1e30
ROPE_BASE = 10000.0
KEY_BLOCK = 512


def rotate(source, places):
    full_width = source.shape[-1]
    half_width = full_width // 2
    inverse = jnp.power(
        jnp.float32(ROPE_BASE), -2.0 * jnp.arange(half_width, dtype=jnp.float32) / full_width
    )
    angles = places.astype(jnp.float32)[:, None] * inverse[None, :]
    cosine = jnp.cos(angles)[:, None, :]
    sine_terms = jnp.sin(angles)[:, None, :]
    first_part = source[..., :half_width].astype(jnp.float32)
    second_part = source[..., half_width:].astype(jnp.float32)
    rotated = jnp.concatenate(
        [
            first_part * cosine - second_part * sine_terms,
            second_part * cosine + first_part * sine_terms,
        ],
        axis=-1,
    )
    return rotated.astype(jnp.bfloat16)


def token_request(token_ids, ends_at):
    return jnp.sum((token_ids[:, None] >= ends_at[None, :]).astype(jnp.int32), axis=1)


def lookup_rows(request, lookup):
    matches = request[:, None] == jnp.arange(lookup.shape[0], dtype=jnp.int32)[None, :]
    return jnp.sum(jnp.where(matches, lookup[None, :], 0), axis=1)


def empty_state(head_count, row_count):
    return (
        jnp.full((head_count, row_count), NEG_FILL, jnp.float32),
        jnp.zeros((head_count, row_count), jnp.float32),
        jnp.zeros((head_count, row_count, HD), jnp.float32),
    )


def finish(running):
    row_best, row_total, summed = running
    head_count, row_count, _ = summed.shape
    return (
        (summed / row_total[:, :, None])
        .transpose(1, 0, 2)
        .reshape(row_count, head_count * HD)
        .astype(jnp.bfloat16)
    )


def update(
    running, query_token_rows, query_tok, query_req, key_rows, value_rows, key_start, ends_at
):
    row_count = key_rows.shape[0]
    head_count = query_token_rows.shape[1]
    key_token_index = key_start + jnp.arange(row_count, dtype=jnp.int32)
    key_req = token_request(key_token_index, ends_at)
    same_request = (key_req[None, :] == query_req[:, None]) & (
        key_token_index[None, :] <= query_tok[:, None]
    )
    prompt_keys = (key_req[None, :] == 0) & (query_req[:, None] != 0)
    allowed = same_request | prompt_keys
    row_best, row_total, summed = running
    key_head_stack = key_rows.reshape(row_count, head_count, HD)
    value_heads = value_rows.reshape(row_count, head_count, HD)
    scores = jnp.einsum(
        "ezq,izq->zei", query_token_rows, key_head_stack, preferred_element_type=jnp.float32
    ) * (1.0 / math.sqrt(HD))
    scores = jnp.where(allowed[None], scores, NEG_FILL)
    best_new = jnp.maximum(row_best, jnp.max(scores, axis=2))
    factor = jnp.exp(row_best - best_new)
    weights = jnp.where(allowed[None], jnp.exp(scores - best_new[:, :, None]), 0.0)
    total_new = row_total * factor + jnp.sum(weights, axis=2)
    mixed = jnp.einsum(
        "eva,ael->evl",
        weights.astype(jnp.bfloat16),
        value_heads,
        preferred_element_type=jnp.float32,
    )
    return (best_new, total_new, summed * factor[:, :, None] + mixed)


def per_device(queries, new_keys, new_values, lengths, offsets, slot_map):
    tok_dev = queries.shape[1]
    local_cols = queries.shape[2]
    head_count = local_cols // HD
    tokens_total = tok_dev * lax.axis_size("seq")
    cache_len = tokens_total // 2
    lengths_row = lengths[0]
    offsets_row = offsets[0]
    slots_row = slot_map[0]
    request_count = lengths_row.shape[0]
    ends_at = jnp.cumsum(lengths_row)
    begins = ends_at - lengths_row
    token_ids = lax.axis_index("seq") * tok_dev + jnp.arange(tok_dev, dtype=jnp.int32)
    request = token_request(token_ids, ends_at)
    places = lookup_rows(request, offsets_row) + token_ids - lookup_rows(request, begins)
    rot_queries = rotate(queries[0].reshape(tok_dev, head_count, HD), places)
    rot_keys = rotate(new_keys[0].reshape(tok_dev, head_count, HD), places).reshape(
        tok_dev, local_cols
    )
    value_rows = new_values[0]
    key_rows = lax.all_gather(rot_keys, "seq", axis=0, tiled=True)
    piece_values = lax.all_gather(value_rows, "seq", axis=0, tiled=True)
    row_count = key_rows.shape[0]

    def key_step(key_index, state_in):
        first_row = key_index * KEY_BLOCK
        return update(
            state_in,
            rot_queries,
            token_ids,
            request,
            lax.dynamic_slice_in_dim(key_rows, first_row, KEY_BLOCK, 0),
            lax.dynamic_slice_in_dim(piece_values, first_row, KEY_BLOCK, 0),
            first_row,
            ends_at,
        )

    finished = lax.fori_loop(0, row_count // KEY_BLOCK, key_step, empty_state(head_count, tok_dev))
    attended = finish(finished)
    stacked = jnp.stack([rot_keys, value_rows])
    my_slot = lax.axis_index("head")
    request_ids = jnp.arange(request_count, dtype=jnp.int32)
    owner = jnp.sum(jnp.where(slots_row == my_slot, request_ids, 0))
    owner_begin = jnp.sum(jnp.where(request_ids == owner, begins, 0))
    slot_of = lookup_rows(request, slots_row)
    member = slot_of[None, :] == request_ids[:, None]
    buckets = jnp.where(member[None, :, :, None], stacked[:, None], jnp.zeros((), jnp.bfloat16))
    moved = lax.all_to_all(
        lax.all_to_all(buckets, "head", split_axis=1, concat_axis=3, tiled=True),
        "seq",
        split_axis=3,
        concat_axis=2,
        tiled=True,
    )
    padded = jnp.concatenate(
        [moved, jnp.zeros((2, 1, cache_len, moved.shape[3]), jnp.bfloat16)], axis=2
    )
    window = lax.dynamic_slice_in_dim(padded, owner_begin, cache_len, 2)
    return (attended[None], window[0:1], window[1:2])


def solution(mesh):
    in_specs = (
        P("rep", "seq", "head"),
        P("rep", "seq", "head"),
        P("rep", "seq", "head"),
        P("rep", None),
        P("rep", None),
        P("rep", None),
    )
    out_specs = (
        P("rep", "seq", "head"),
        P("rep", "head", None, "seq"),
        P("rep", "head", None, "seq"),
    )
    return jax.shard_map(
        per_device, mesh=mesh, in_specs=in_specs, out_specs=out_specs, check_vma=False
    )
```

profile of v0, /device:TPU:96, one launch (start us, length us, event | category | flops | bytes accessed | tf_op | source)
XLA Modules:
  0.0 385.8 jit_solution(3452643616625133445)
XLA Ops:
  7.2 0.0 all-gather.4.cloned.1.call-start
  7.3 0.9 reduce-window.4
  8.1 0.7 fusion.29
  8.8 1.5 copy.46
  10.3 0.1 convert_reduce_fusion.1
  10.4 0.8 select_reduce_fusion
  11.1 0.5 multiply_cosine_fusion
  11.6 0.3 fusion.21
  11.9 1.0 maximum_convert_fusion
  12.9 0.0 all-gather.4.cloned.1.call-update
  12.9 0.0 all-gather.6.cloned.1.call-start
  13.0 1.3 copy.48
  14.3 0.0 all-gather.6.cloned.1.call-update
  14.3 0.6 copy.49
  14.9 1.4 pad_maximum_fusion
  16.3 2.8 copy.50
  19.1 3.4 broadcast_select_fusion
  22.6 5.6 %all-to-all-start = ((bf16[2,4,256,1792]{2,3,0,1:T(8,128)(2,1)}), bf16[2,4,256,1792]{2,3,0,1:T(8,128)(2,1)}, u32[]{:S(2)}, u32[]{:S(2)}) async-start(bf16[2,4,256,1792]{2,3,0,1:T(8,128)(2,1)} %broadcast_select_fusion), calls=%async_computation | async-start | bytes 14680064 | tf_op jit(solution)/shard_map/all_to_all | solution.py:142
  28.2 0.5 copy.47
  28.8 0.7 fusion.27
  29.5 0.0 copy-done.4
  29.5 1.3 fusion.28
  32.6 0.3 fusion.24
  32.9 0.1 pad_maximum_fusion.1
  33.0 78.6 %all-to-all-done = bf16[2,4,256,1792]{2,3,0,1:T(8,128)(2,1)} async-done(((bf16[2,4,256,1792]{2,3,0,1:T(8,128)(2,1)}), bf16[2,4,256,1792]{2,3,0,1:T(8,128)(2,1)}, u32[]{:S(2)}, u32[]{:S(2)}) %all-to-all-start) | async-done | bytes 7340064 | tf_op jit(solution)/shard_map/all_to_all | solution.py:142
  111.6 3.6 copy.51
  115.2 47.2 %copy.52 = bf16[2,1,256,7168]{2,0,1,3:T(2,128)(2,1)} copy(bf16[2,1,256,7168]{2,3,0,1:T(8,128)(2,1)S(1)} %bitcast.73) | data formatting | bytes 14680064 | tf_op jit(solution)/shard_map/all_to_all | solution.py:142
  162.3 7.7 %all-to-all-start.1 = ((bf16[2,1,256,7168]{2,0,1,3:T(2,128)(2,1)}), bf16[2,1,256,7168]{2,0,1,3:T(2,128)(2,1)}, u32[]{:S(2)}, u32[]{:S(2)}) async-start(bf16[2,1,256,7168]{2,0,1,3:T(2,128)(2,1)} %copy.52), calls=%async_computation.1 | async-start | bytes 14680064 | tf_op jit(solution)/shard_map/all_to_all | solution.py:141
  170.0 106.1 %all-gather.6.cloned.1.call-done = bf16[1,2048,1792]{1,2,0:T(8,128)(2,1)} async-done(((bf16[1,256,1792]{1,2,0:T(8,128)(2,1)}), bf16[1,2048,1792]{1,2,0:T(8,128)(2,1)}) %all-gather.6.cloned.1.call-update) | async-done | bytes 7340048 | tf_op jit(solution)/shard_map/all_gather | solution.py:115
  276.2 51.9 %while.18 = (s32[]{:T(128)}, f32[8,256]{1,0:T(8,128)S(1)}, f32[8,256]{1,0:T(8,128)S(1)}, f32[8,256,224]{1,2,0:T(8,128)}, s32[4]{0:T(128)S(1)}, /*index=5*/s32[25...) while((s32[]{:T(128)}, f32[8,256]{1,0:T(8,128)S(1)}, ...), condition=%wide.region_8.9_spmd.clone, body=%wide.region_4.8_spmd.clone.sunk | while | flops 955204608 | bytes 45631228 | solution.py:131
  276.2 0.1 convert_reduce_fusion.3
  276.3 0.3 and_or_fusion.2
  276.6 2.3 constant_dynamic-slice_fusion.3
  278.9 3.1 fusion.45
  281.9 3.3 fusion.46
  285.3 0.1 copy-done
  285.4 2.6 fusion.48
  288.0 0.1 convert_reduce_fusion.3
  288.1 0.3 and_or_fusion.2
  288.4 2.3 constant_dynamic-slice_fusion.3
  290.7 3.1 fusion.45
  293.8 3.3 fusion.46
  297.2 0.1 copy-done
  297.2 4.1 %fusion.48 = f32[8,256,224]{1,2,0:T(8,128)} fusion(f32[8,256,224]{1,2,0:T(8,128)} %get-tuple-element.350, bf16[512,8,224]{0,2,1:T(8,128)(2,1)S(1)} %bitcast.71, f32[8,512,256]{2,1,0:T(8,128)S(1)} %copy-done, f32[8,256]{1,0:T(8,128)S(1)} %select_maximum_fusion.2, pred[256,512]{0,1:T(8,128)(4,1)S(1)} %and_or_fusion.2, ...), kind=kOutput, calls=%fused_computation.13.clone.1 | convolution fusion | flops 476381184 | bytes 9846785 | tf_op jit(solution)/shard_map/while/body/eval_jaxpr/eva,ael->evl/dot_general | solution.py:85
  301.4 0.1 convert_reduce_fusion.3
  301.5 0.3 and_or_fusion.2
  301.8 2.3 constant_dynamic-slice_fusion.3
  304.1 3.1 fusion.45
  307.2 3.3 fusion.46
  310.5 0.1 copy-done
  310.6 4.1 %fusion.48 = f32[8,256,224]{1,2,0:T(8,128)} fusion(f32[8,256,224]{1,2,0:T(8,128)} %get-tuple-element.350, bf16[512,8,224]{0,2,1:T(8,128)(2,1)S(1)} %bitcast.71, f32[8,512,256]{2,1,0:T(8,128)S(1)} %copy-done, f32[8,256]{1,0:T(8,128)S(1)} %select_maximum_fusion.2, pred[256,512]{0,1:T(8,128)(4,1)S(1)} %and_or_fusion.2, ...), kind=kOutput, calls=%fused_computation.13.clone.1 | convolution fusion | flops 476381184 | bytes 9846785 | tf_op jit(solution)/shard_map/while/body/eval_jaxpr/eva,ael->evl/dot_general | solution.py:85
  314.7 0.1 convert_reduce_fusion.3
  314.8 0.3 and_or_fusion.2
  315.1 2.3 constant_dynamic-slice_fusion.3
  317.4 3.1 fusion.45
  320.5 3.3 fusion.46
  323.9 0.1 copy-done
  323.9 4.1 %fusion.48 = f32[8,256,224]{1,2,0:T(8,128)} fusion(f32[8,256,224]{1,2,0:T(8,128)} %get-tuple-element.350, bf16[512,8,224]{0,2,1:T(8,128)(2,1)S(1)} %bitcast.71, f32[8,512,256]{2,1,0:T(8,128)S(1)} %copy-done, f32[8,256]{1,0:T(8,128)S(1)} %select_maximum_fusion.2, pred[256,512]{0,1:T(8,128)(4,1)S(1)} %and_or_fusion.2, ...), kind=kOutput, calls=%fused_computation.13.clone.1 | convolution fusion | flops 476381184 | bytes 9846785 | tf_op jit(solution)/shard_map/while/body/eval_jaxpr/eva,ael->evl/dot_general | solution.py:85
  328.1 1.6 divide_convert_fusion
  329.7 1.4 copy.55
  331.1 24.2 %all-to-all-done.1 = bf16[2,1,256,7168]{2,0,1,3:T(2,128)(2,1)} async-done(((bf16[2,1,256,7168]{2,0,1,3:T(2,128)(2,1)}), bf16[2,1,256,7168]{2,0,1,3:T(2,128)(2,1)}, u32[]{:S(2)}, u32[]{:S(2)}) %all-to-all-start.1) | async-done | bytes 7340064 | tf_op jit(solution)/shard_map/all_to_all | solution.py:141
  355.3 7.0 %copy.53 = bf16[2,1,256,7168]{2,3,0,1:T(8,128)(2,1)} copy(bf16[2,1,256,7168]{2,0,1,3:T(2,128)(2,1)} %all-to-all-done.1) | data formatting | bytes 14680064 | tf_op jit(solution)/shard_map/all_to_all | solution.py:141
  362.3 11.1 %copy.54 = bf16[2,1,8,256,896]{4,3,2,0,1:T(8,128)(2,1)} copy(bf16[2,1,8,256,896]{3,4,2,0,1:T(8,128)(2,1)} %bitcast.74) | data formatting | bytes 14680064 | tf_op jit(solution)/shard_map/all_to_all | solution.py:141
  373.4 5.6 %fusion.19 = (bf16[1,1,1024,896]{3,2,1,0:T(8,128)(2,1)}, bf16[1,1,1024,896]{3,2,1,0:T(8,128)(2,1)}) fusion(s32[]{:T(128)S(6)} %add.111, s32[]{:T(128)S(6)} %select_n.53, bf16[2,1,2048,896]{3,2,0,1:T(8,128)(2,1)} %bitcast.75), kind=kLoop, calls=%fused_computation.32 | loop fusion | bytes 11010056
  (49 shorter events, 0.2 us)
Async XLA Ops:
  7.2 5.8 %copy-start.2 = (bf16[1,256,1792]{2,1,0:T(8,128)(2,1)S(1)}, bf16[1,256,1792]{2,1,0:T(8,128)(2,1)}, u32[]{:S(2)}) copy-start(bf16[1,256,1792]{2,1,0:T(8,128)(2,1)} %param.10) | copy-start | bytes 2752516
  7.2 162.8 %all-gather.4.cloned.1.call-start = ((), (), s32[]{:S(2)}) async-start(), calls=%async_computation.2 | async-start | bytes 8257536 | tf_op jit(solution)/shard_map/all_gather | solution.py:114
  12.9 1.4 copy-start.1
  12.9 263.2 %all-gather.6.cloned.1.call-start = ((), (), s32[]{:S(2)}) async-start(), calls=%async_computation.3 | async-start | bytes 8257536 | tf_op jit(solution)/shard_map/all_gather | solution.py:115
  22.6 5.6 %copy-start.3 = (bf16[1,256,1792]{2,1,0:T(8,128)(2,1)S(1)}, bf16[1,256,1792]{2,1,0:T(8,128)(2,1)}, u32[]{:S(2)}) copy-start(bf16[1,256,1792]{2,1,0:T(8,128)(2,1)} %param.8) | copy-start | bytes 2752516
  22.6 6.2 %copy-start.5 = (s32[1,4]{1,0:T(1,128)S(1)}, s32[1,4]{1,0:T(1,128)}, u32[]{:S(2)}) copy-start(s32[1,4]{1,0:T(1,128)} %param.13) | copy-start | bytes 52
  22.6 6.9 %copy-start.4 = (s32[1,4]{1,0:T(1,128)S(1)}, s32[1,4]{1,0:T(1,128)}, u32[]{:S(2)}) copy-start(s32[1,4]{1,0:T(1,128)} %param.11) | copy-start | bytes 52
  22.6 89.0 %all-to-all-start = ((bf16[2,4,256,1792]{2,3,0,1:T(8,128)(2,1)}), bf16[2,4,256,1792]{2,3,0,1:T(8,128)(2,1)}, u32[]{:S(2)}, u32[]{:S(2)}) async-start(bf16[2,4,256,1792]{2,3,0,1:T(8,128)(2,1)} %broadcast_select_fusion), calls=%async_computation | async-start | bytes 14680064 | tf_op jit(solution)/shard_map/all_to_all | solution.py:142
  162.3 192.9 %all-to-all-start.1 = ((bf16[2,1,256,7168]{2,0,1,3:T(2,128)(2,1)}), bf16[2,1,256,7168]{2,0,1,3:T(2,128)(2,1)}, u32[]{:S(2)}, u32[]{:S(2)}) async-start(bf16[2,1,256,7168]{2,0,1,3:T(2,128)(2,1)} %copy.52), calls=%async_computation.1 | async-start | bytes 14680064 | tf_op jit(solution)/shard_map/all_to_all | solution.py:141
  281.9 3.4 copy-start
  293.8 3.4 copy-start
  307.1 3.4 copy-start
  320.5 3.4 copy-start
Sparse Core Ops, SparseCore 0:
  13.1 91.4 all-gather.3
  106.8 169.2 all-gather.5
where the time goes:
time: 387 us; the launch traced here: 386 us
  waiting for transfers between devices  209 us (54%)
  local copies, waits for them, and re-layouts  92 us (24%)
  other arithmetic  28 us (7%)
  matrix products  27.3 us (7%)
  between operations  16.1 us (4%)
  starting transfers between devices  13.3 us (3%)
    all_gather x1, waiting for transfers between devices, per_device(): piece_values = lax.all_gather(value_rows, 'seq', axis=0, tiled=True)  106 us
    all_to_all x1, waiting for transfers between devices, per_device(): lax.all_to_all(buckets, 'head', split_axis=1, concat_axis=3, tiled=True)  78.6 us
    all_to_all x2, local copies, waits for them, and re-layouts, per_device(): lax.all_to_all(buckets, 'head', split_axis=1, concat_axis=3, tiled=True)  50.7 us
    all_to_all x1, waiting for transfers between devices, per_device(): lax.all_to_all(lax.all_to_all(buckets, 'head', split_axis=1, concat_axis=...  24.2 us
    all_to_all x2, local copies, waits for them, and re-layouts, per_device(): lax.all_to_all(lax.all_to_all(buckets, 'head', split_axis=1, concat_axis=...  18.1 us
    dot_general x4, matrix products, update(): jnp.einsum('eva,ael->evl', weights.astype(jnp.bfloat16), value_heads, pre...  15 us
    reduce_sum x4, other arithmetic, update(): total_new = row_total * factor + jnp.sum(weights, axis=2)  13.3 us
    dot_general x4, matrix products, update(): jnp.einsum('ezq,izq->zei', query_token_rows, key_head_stack, preferred_el...  12.3 us
  transfers between devices with their start and end apart: 4, of which 3 were waited for; matrix products, arithmetic and copies ran while one was open for 31% of the time, Pallas kernels for 0%

commit v1 on v0

--- a/solution.py
+++ b/solution.py
@@ -138,12 +138,14 @@
     slot_of = lookup_rows(request, slots_row)
     member = slot_of[None, :] == request_ids[:, None]
     buckets = jnp.where(member[None, :, :, None], stacked[:, None], jnp.zeros((), jnp.bfloat16))
-    moved = lax.all_to_all(
-        lax.all_to_all(buckets, "head", split_axis=1, concat_axis=3, tiled=True),
-        "seq",
-        split_axis=3,
-        concat_axis=2,
-        tiled=True,
+    link_cube = lambda array_here, across: jnp.concatenate(
+        lax.all_to_all(
+            jnp.stack(jnp.split(array_here, lax.axis_size(across), axis=3), axis=0), across, 0, 0
+        ),
+        axis=2,
+    )
+    moved = link_cube(
+        lax.all_to_all(buckets, "head", split_axis=1, concat_axis=3, tiled=True), "seq"
     )
     padded = jnp.concatenate(
         [moved, jnp.zeros((2, 1, cache_len, moved.shape[3]), jnp.bfloat16)], axis=2

time: 387 us -> 405 us (1.047)
  the two profiles are of different devices: /device:TPU:96 before, /device:TPU:50 now
where the time goes in v1:
time: 405 us; the launch traced here: 404 us
  waiting for transfers between devices  262 us (65%)
  local copies, waits for them, and re-layouts  57.2 us (14%)
  matrix products  27.3 us (7%)
  other arithmetic  26.8 us (7%)
  between operations  16 us (4%)
  starting transfers between devices  14.6 us (4%)
    all_gather x1, waiting for transfers between devices, per_device(): piece_values = lax.all_gather(value_rows, 'seq', axis=0, tiled=True)  186 us
    all_to_all x1, waiting for transfers between devices, per_device(): lax.all_to_all(buckets, 'head', split_axis=1, concat_axis=3, tiled=True)  75.5 us
    unnamed x24, local copies, waits for them, and re-layouts  20.9 us
    dot_general x4, matrix products, update(): jnp.einsum('eva,ael->evl', weights.astype(jnp.bfloat16), value_heads, pre...  15 us
    reduce_sum x4, other arithmetic, update(): total_new = row_total * factor + jnp.sum(weights, axis=2)  13.3 us
    another operation x2, local copies, waits for them, and re-layouts, per_device(): jnp.stack(jnp.split(array_here, lax.axis_size(across), axis=3), axis=0)  12.3 us
    dot_general x4, matrix products, update(): jnp.einsum('ezq,izq->zei', query_token_rows, key_head_stack, preferred_el...  12.3 us
    all_to_all x1, local copies, waits for them, and re-layouts, per_device(): lax.all_to_all(buckets, 'head', split_axis=1, concat_axis=3, tiled=True)  10.1 us
  transfers between devices with their start and end apart: 4, of which 2 were waited for; matrix products, arithmetic and copies ran while one was open for 24% of the time, Pallas kernels for 0%

profile of v1, /device:TPU:50, one launch (start us, length us, event | category | flops | bytes accessed | tf_op | source)
XLA Modules:
  0.0 403.7 jit_solution(6367399967083453207)
XLA Ops:
  7.3 0.9 reduce-window.4
  8.1 0.7 fusion.37
  8.8 1.5 copy.53
  10.3 0.1 convert_reduce_fusion.1
  10.4 0.8 select_reduce_fusion
  11.1 0.5 multiply_cosine_fusion
  11.6 0.3 fusion.21
  11.9 1.0 maximum_convert_fusion
  13.0 1.3 copy.55
  14.3 0.6 copy.56
  15.0 0.2 pad_maximum_fusion
  15.1 3.5 broadcast_select_fusion
  18.6 5.9 %all-to-all-start = ((bf16[2,4,256,1792]{3,2,0,1:T(8,128)(2,1)}), bf16[2,4,256,1792]{3,2,0,1:T(8,128)(2,1)}, u32[]{:S(2)}, u32[]{:S(2)}) async-start(bf16[2,4,256,1792]{3,2,0,1:T(8,128)(2,1)} %broadcast_select_fusion), calls=%async_computation | async-start | bytes 14680064 | tf_op jit(solution)/shard_map/all_to_all | solution.py:148
  24.5 0.5 copy.54
  25.1 0.7 fusion.35
  25.8 1.3 fusion.36
  28.9 0.3 fusion.24
  29.3 0.1 pad_maximum_fusion.1
  29.3 75.5 %all-to-all-done = bf16[2,4,256,1792]{3,2,0,1:T(8,128)(2,1)} async-done(((bf16[2,4,256,1792]{3,2,0,1:T(8,128)(2,1)}), bf16[2,4,256,1792]{3,2,0,1:T(8,128)(2,1)}, u32[]{:S(2)}, u32[]{:S(2)}) %all-to-all-start) | async-done | bytes 7340064 | tf_op jit(solution)/shard_map/all_to_all | solution.py:148
  104.9 10.1 %copy.57 = bf16[2,4,256,1792]{2,3,1,0:T(8,128)(2,1)} copy(bf16[2,4,256,1792]{3,2,0,1:T(8,128)(2,1)} %all-to-all-done) | data formatting | bytes 14680064 | tf_op jit(solution)/shard_map/all_to_all | solution.py:148
  114.9 2.3 fusion.34
  117.2 2.5 fusion.33
  119.8 2.2 fusion.32
  122.0 2.3 fusion.31
  124.3 1.1 fusion.30
  125.3 1.0 fusion.29
  126.3 1.0 fusion.28
  127.3 1.0 fusion.27
  128.3 11.3 %copy.58 = bf16[8,2,1,256,896]{4,3,1,2,0:T(8,128)(2,1)} copy(bf16[8,2,1,256,896]{3,4,1,2,0:T(8,128)(2,1)} %fusion.27) | data formatting | bytes 14680064 | tf_op jit(solution)/shard_map/stack | solution.py:143
  139.6 8.6 %all-to-all-start.1 = ((bf16[8,2,1,256,896]{4,3,1,2,0:T(8,128)(2,1)}), bf16[8,2,1,256,896]{4,3,1,2,0:T(8,128)(2,1)}, u32[]{:S(2)}, u32[]{:S(2)}) async-start(bf16[8,2,1,256,896]{4,3,1,2,0:T(8,128)(2,1)} %copy.58), calls=%async_computation.1 | async-start | bytes 14680064 | tf_op jit(solution)/shard_map/all_to_all | solution.py:142
  148.2 186.1 %all-gather.6.cloned.1.call-done = bf16[1,2048,1792]{1,2,0:T(8,128)(2,1)} async-done(((bf16[1,256,1792]{1,2,0:T(8,128)(2,1)}), bf16[1,2048,1792]{1,2,0:T(8,128)(2,1)}) %all-gather.6.cloned.1.call-update) | async-done | bytes 7340048 | tf_op jit(solution)/shard_map/all_gather | solution.py:115
  334.3 51.9 %while.18 = (s32[]{:T(128)}, f32[8,256]{1,0:T(8,128)S(1)}, f32[8,256]{1,0:T(8,128)S(1)}, f32[8,256,224]{1,2,0:T(8,128)}, s32[4]{0:T(128)S(1)}, /*index=5*/s32[25...) while((s32[]{:T(128)}, f32[8,256]{1,0:T(8,128)S(1)}, ...), condition=%wide.region_8.9_spmd.clone, body=%wide.region_4.8_spmd.clone.sunk | while | flops 955204608 | bytes 45631228 | solution.py:131
  334.3 0.1 convert_reduce_fusion.3
  334.4 0.3 and_or_fusion.2
  334.7 2.3 constant_dynamic-slice_fusion.3
  337.0 3.1 fusion.53
  340.0 3.3 fusion.54
  343.4 0.1 copy-done
  343.5 2.6 fusion.56
  346.1 0.1 convert_reduce_fusion.3
  346.2 0.3 and_or_fusion.2
  346.5 2.3 constant_dynamic-slice_fusion.3
  348.8 3.1 fusion.53
  351.9 3.3 fusion.54
  355.3 0.1 copy-done
  355.3 4.1 %fusion.56 = f32[8,256,224]{1,2,0:T(8,128)} fusion(f32[8,256,224]{1,2,0:T(8,128)} %get-tuple-element.350, bf16[512,8,224]{0,2,1:T(8,128)(2,1)S(1)} %bitcast.102, f32[8,512,256]{2,1,0:T(8,128)S(1)} %copy-done, f32[8,256]{1,0:T(8,128)S(1)} %select_maximum_fusion.2, pred[256,512]{0,1:T(8,128)(4,1)S(1)} %and_or_fusion.2, ...), kind=kOutput, calls=%fused_computation.13.clone.1 | convolution fusion | flops 476381184 | bytes 9846785 | tf_op jit(solution)/shard_map/while/body/eval_jaxpr/eva,ael->evl/dot_general | solution.py:85
  359.5 0.1 convert_reduce_fusion.3
  359.6 0.3 and_or_fusion.2
  359.9 2.3 constant_dynamic-slice_fusion.3
  362.2 3.1 fusion.53
  365.3 3.3 fusion.54
  368.6 0.1 copy-done
  368.7 4.1 %fusion.56 = f32[8,256,224]{1,2,0:T(8,128)} fusion(f32[8,256,224]{1,2,0:T(8,128)} %get-tuple-element.350, bf16[512,8,224]{0,2,1:T(8,128)(2,1)S(1)} %bitcast.102, f32[8,512,256]{2,1,0:T(8,128)S(1)} %copy-done, f32[8,256]{1,0:T(8,128)S(1)} %select_maximum_fusion.2, pred[256,512]{0,1:T(8,128)(4,1)S(1)} %and_or_fusion.2, ...), kind=kOutput, calls=%fused_computation.13.clone.1 | convolution fusion | flops 476381184 | bytes 9846785 | tf_op jit(solution)/shard_map/while/body/eval_jaxpr/eva,ael->evl/dot_general | solution.py:85
  372.8 0.1 convert_reduce_fusion.3
  372.9 0.3 and_or_fusion.2
  373.2 2.3 constant_dynamic-slice_fusion.3
  375.5 3.1 fusion.53
  378.6 3.3 fusion.54
  382.0 0.1 copy-done
  382.0 4.1 %fusion.56 = f32[8,256,224]{1,2,0:T(8,128)} fusion(f32[8,256,224]{1,2,0:T(8,128)} %get-tuple-element.350, bf16[512,8,224]{0,2,1:T(8,128)(2,1)S(1)} %bitcast.102, f32[8,512,256]{2,1,0:T(8,128)S(1)} %copy-done, f32[8,256]{1,0:T(8,128)S(1)} %select_maximum_fusion.2, pred[256,512]{0,1:T(8,128)(4,1)S(1)} %and_or_fusion.2, ...), kind=kOutput, calls=%fused_computation.13.clone.1 | convolution fusion | flops 476381184 | bytes 9846785 | tf_op jit(solution)/shard_map/while/body/eval_jaxpr/eva,ael->evl/dot_general | solution.py:85
  386.2 1.6 divide_convert_fusion
  387.8 1.4 copy.60
  389.2 3.9 copy.59
  393.1 3.8 fusion.19
  (57 shorter events, 0.3 us)
Async XLA Ops:
  7.2 5.8 %copy-start.3 = (bf16[1,256,1792]{2,1,0:T(8,128)(2,1)S(1)}, bf16[1,256,1792]{2,1,0:T(8,128)(2,1)}, u32[]{:S(2)}) copy-start(bf16[1,256,1792]{2,1,0:T(8,128)(2,1)} %param.10) | copy-start | bytes 2752516
  7.2 141.0 %all-gather.4.cloned.1.call-start = ((), (), s32[]{:S(2)}) async-start(), calls=%async_computation.2 | async-start | bytes 8257536 | tf_op jit(solution)/shard_map/all_gather | solution.py:114
  12.9 1.4 copy-start.2
  12.9 321.3 %all-gather.6.cloned.1.call-start = ((), (), s32[]{:S(2)}) async-start(), calls=%async_computation.3 | async-start | bytes 8257536 | tf_op jit(solution)/shard_map/all_gather | solution.py:115
  18.6 5.9 %copy-start.4 = (bf16[1,256,1792]{2,1,0:T(8,128)(2,1)S(1)}, bf16[1,256,1792]{2,1,0:T(8,128)(2,1)}, u32[]{:S(2)}) copy-start(bf16[1,256,1792]{2,1,0:T(8,128)(2,1)} %param.8) | copy-start | bytes 2752516
  18.6 6.4 %copy-start.6 = (s32[1,4]{1,0:T(1,128)S(1)}, s32[1,4]{1,0:T(1,128)}, u32[]{:S(2)}) copy-start(s32[1,4]{1,0:T(1,128)} %param.13) | copy-start | bytes 52
  18.6 7.2 %copy-start.5 = (s32[1,4]{1,0:T(1,128)S(1)}, s32[1,4]{1,0:T(1,128)}, u32[]{:S(2)}) copy-start(s32[1,4]{1,0:T(1,128)} %param.11) | copy-start | bytes 52
  18.6 86.2 %all-to-all-start = ((bf16[2,4,256,1792]{3,2,0,1:T(8,128)(2,1)}), bf16[2,4,256,1792]{3,2,0,1:T(8,128)(2,1)}, u32[]{:S(2)}, u32[]{:S(2)}) async-start(bf16[2,4,256,1792]{3,2,0,1:T(8,128)(2,1)} %broadcast_select_fusion), calls=%async_computation | async-start | bytes 14680064 | tf_op jit(solution)/shard_map/all_to_all | solution.py:148
  114.9 9.3 %copy-start.1 = (bf16[2,4,256,1792]{2,3,1,0:T(8,128)(2,1)S(1)}, bf16[2,4,256,1792]{2,3,1,0:T(8,128)(2,1)}, u32[]{:S(2)}) copy-start(bf16[2,4,256,1792]{2,3,1,0:T(8,128)(2,1)} %copy.57) | copy-start | bytes 22020100
  139.6 249.6 %all-to-all-start.1 = ((bf16[8,2,1,256,896]{4,3,1,2,0:T(8,128)(2,1)}), bf16[8,2,1,256,896]{4,3,1,2,0:T(8,128)(2,1)}, u32[]{:S(2)}, u32[]{:S(2)}) async-start(bf16[8,2,1,256,896]{4,3,1,2,0:T(8,128)(2,1)} %copy.58), calls=%async_computation.1 | async-start | bytes 14680064 | tf_op jit(solution)/shard_map/all_to_all | solution.py:142
  340.0 3.4 copy-start
  351.9 3.4 copy-start
  365.2 3.4 copy-start
  378.6 3.4 copy-start
Sparse Core Ops, SparseCore 0:
  13.1 92.7 all-gather.3
  108.1 226.1 all-gather.5
